TPU v7x, 512 devices: a whole 4x8x8 slice. The times are simulated.
512 devices in a mesh: dp: 2 (over core), ctx: 64 (over z, y), head: 4 (over x).
Axes of the slice: x: 4, y: 8, z: 8, core: 2. Of those that a mesh axis runs over, the one named last changes fastest.
Arguments:
- queries: bfloat16 [2, 8192, 2560], P('dp', 'ctx', 'head'), may hold values from -25 to 25
- keys: bfloat16 [2, 8192, 2560], P('dp', 'ctx', 'head'), may hold values from -25 to 25
- values: bfloat16 [2, 8192, 2560], P('dp', 'ctx', 'head'), may hold values from -6 to 6
- grad_y: bfloat16 [2, 8192, 2560], P('dp', 'ctx', 'head'), may hold values from -6 to 6
- out_gain: float32 [2560], P('head'), may hold values from 0.1 to 1.9
- offsets: int32 [2, 20], P(None, 'head'), may hold values from 0 to 63, as said below
Outputs:
- attended: bfloat16 [2, 8192, 2560], P('dp', 'ctx', 'head')
- query_grad: bfloat16 [2, 8192, 2560], P('dp', 'ctx', 'head')
- key_grad: bfloat16 [2, 8192, 2560], P('dp', 'ctx', 'head')
- value_grad: bfloat16 [2, 8192, 2560], P('dp', 'ctx', 'head')
- gain_grad: float32 [2560], P('head')
Inputs may be any that keep to these rules, and one draw needn't show every extreme that they name: Row 0 holds offsets below 8, row 1 offsets below 64.
All inputs are finite; a program needn't handle non-finite values.
Results may differ from a plain program's by a relative error of at most 0.011.
Values may be sent and summed in bfloat16 or wider, within the bound.
A program may use at most 64 MiB of HBM per device.

v0:
```python
import math
import jax
import jax.numpy as jnp
from jax import lax
from jax.sharding import PartitionSpec as P

HEAD_DIM = 128
SPAN = 4
R1 = 8
EPS = 1e-06


def swapped(block, axis, bit):
    count = lax.axis_size(axis)
    route = []
    for low in range(count):
        high = low | 1 << bit
        if high != low and high < count:
            route += [(low, high), (high, low)]
    return lax.ppermute(block, axis, route)


def pick_rows(source_rows, dilation, shifts):
    row_count, head_count, head_width = source_rows.shape
    grouped = source_rows.reshape(row_count // dilation, dilation, head_count, head_width)
    hit_mask = jnp.arange(dilation, dtype=jnp.int32).reshape(1, dilation, 1, 1) == shifts.reshape(
        1, 1, head_count, 1
    )
    chosen = jnp.where(hit_mask, grouped, jnp.zeros((), source_rows.dtype))
    return jnp.sum(chosen, axis=1, dtype=source_rows.dtype)


def place_rows(row_values, dilation, shifts):
    row_count, head_count, head_width = row_values.shape
    hit_mask = jnp.arange(dilation, dtype=jnp.int32).reshape(1, dilation, 1, 1) == shifts.reshape(
        1, 1, head_count, 1
    )
    spread = jnp.where(hit_mask, row_values[:, None], jnp.zeros((), row_values.dtype))
    return spread.reshape(row_count * dilation, head_count, head_width)


def level_scores(q_rows, k_rows):
    score_scale = 1.0 / math.sqrt(q_rows.shape[-1])
    return (
        jnp.einsum("qhe,khe->hqk", q_rows, k_rows, preferred_element_type=jnp.float32) * score_scale
    )


def attend(q_rows, k_rows, v_rows):
    scores = level_scores(q_rows, k_rows)
    row_max = jnp.max(scores, axis=-1, keepdims=True)
    log_total = row_max[..., 0] + jnp.log(jnp.sum(jnp.exp(scores - row_max), axis=-1))
    soft_rows = jnp.exp(scores - log_total[..., None]).astype(jnp.bfloat16)
    level_out = jnp.einsum("hqk,khe->qhe", soft_rows, v_rows, preferred_element_type=jnp.float32)
    return (level_out, log_total.T)


def score_grads(q_rows, k_rows, v_rows, log_total, grad_low, row_shift):
    score_scale = 1.0 / math.sqrt(q_rows.shape[-1])
    scores = level_scores(q_rows, k_rows)
    exact_soft = jnp.exp(scores - log_total.T[..., None])
    prob_grad = jnp.einsum("qhe,khe->hqk", grad_low, v_rows, preferred_element_type=jnp.float32)
    score_grad = (exact_soft * (prob_grad + row_shift.T[..., None]) * score_scale).astype(
        jnp.bfloat16
    )
    return (score_grad, exact_soft.astype(jnp.bfloat16))


def key_parts(score_grad, soft_low, q_rows, grad_low):
    k_part = jnp.einsum("hqk,qhe->khe", score_grad, q_rows, preferred_element_type=jnp.float32)
    v_part = jnp.einsum("hqk,qhe->khe", soft_low, grad_low, preferred_element_type=jnp.float32)
    return (k_part, v_part)


def query_part(score_grad, k_rows):
    return jnp.einsum("hqk,khe->qhe", score_grad, k_rows, preferred_element_type=jnp.float32)


def shards(queries, keys, values, grad_y, out_gain, offsets):
    tokens = queries.shape[1]
    flat_width = queries.shape[2]
    head_count = flat_width // HEAD_DIM
    row_shape = (tokens, head_count, HEAD_DIM)
    q_own = queries[0].reshape(row_shape)
    k_own = keys[0].reshape(row_shape)
    v_own = values[0].reshape(row_shape)
    ctx_size = lax.axis_size("ctx")
    span_bits = SPAN.bit_length() - 1
    my_place = lax.axis_index("ctx")
    mid_shift = offsets[0]
    top_shift = offsets[1]
    positions = jnp.arange(tokens, dtype=jnp.int32)
    mid_hit = (positions % R1)[:, None] == mid_shift[None, :]
    top_hit = (positions % ctx_size)[:, None] == top_shift[None, :]
    mid_q = pick_rows(q_own, R1, mid_shift)
    mid_k = pick_rows(k_own, R1, mid_shift)
    mid_v = pick_rows(v_own, R1, mid_shift)
    top_q = pick_rows(q_own, ctx_size, top_shift)
    top_k = pick_rows(k_own, ctx_size, top_shift)
    top_v = pick_rows(v_own, ctx_size, top_shift)
    mid_keys = mid_k.reshape(-1, flat_width)
    mid_vals = mid_v.reshape(-1, flat_width)
    top_keys = top_k.reshape(-1, flat_width)
    top_vals = top_v.reshape(-1, flat_width)

    def append_peer(mine, received, level_bit):
        upper_side = my_place >> level_bit & 1 == 1
        return jnp.where(
            upper_side, jnp.concatenate([received, mine], 0), jnp.concatenate([mine, received], 0)
        )

    for level_bit in range(span_bits):
        received = swapped((mid_keys, mid_vals), "ctx", level_bit)
        mid_keys = append_peer(mid_keys, received[0], level_bit)
        mid_vals = append_peer(mid_vals, received[1], level_bit)
    top_keys, top_vals = (
        lax.all_gather(top_keys, "ctx", axis=0, tiled=True),
        lax.all_gather(top_vals, "ctx", axis=0, tiled=True),
    )
    mid_keys = mid_keys.reshape(-1, head_count, HEAD_DIM)
    mid_vals = mid_vals.reshape(-1, head_count, HEAD_DIM)
    top_keys = top_keys.reshape(-1, head_count, HEAD_DIM)
    top_vals = top_vals.reshape(-1, head_count, HEAD_DIM)
    base_out, base_total = attend(q_own, k_own, v_own)
    mid_out, mid_total = attend(mid_q, mid_keys, mid_vals)
    top_out, top_total = attend(top_q, top_keys, top_vals)
    mid_full = place_rows(mid_total[..., None], R1, mid_shift)[..., 0]
    top_full = place_rows(top_total[..., None], ctx_size, top_shift)[..., 0]
    row_max = jnp.maximum(base_total, jnp.where(mid_hit, mid_full, base_total))
    row_max = jnp.maximum(row_max, jnp.where(top_hit, top_full, base_total))
    base_expo = jnp.exp(base_total - row_max)
    mid_expo = jnp.where(mid_hit, jnp.exp(mid_full - row_max), 0.0)
    top_expo = jnp.where(top_hit, jnp.exp(top_full - row_max), 0.0)
    denom = base_expo + mid_expo + top_expo
    base_share = base_expo / denom
    mid_share = mid_expo / denom
    top_share = top_expo / denom
    attn = (
        base_share[..., None] * base_out
        + mid_share[..., None] * place_rows(mid_out, R1, mid_shift)
        + top_share[..., None] * place_rows(top_out, ctx_size, top_shift)
    )
    inv_rms = lax.rsqrt(jnp.mean(attn * attn, axis=-1, keepdims=True) + EPS)
    normed = attn * inv_rms
    gain_rows = out_gain.reshape(head_count, HEAD_DIM)
    attended = (normed * gain_rows).astype(jnp.bfloat16).reshape(1, tokens, flat_width)
    grad_full = grad_y[0].reshape(row_shape).astype(jnp.float32)
    gain_part = jnp.sum(grad_full * normed, axis=0).reshape(flat_width)
    gain_grad = lax.psum(gain_part, ("dp", "ctx"))
    grad_norm = grad_full * gain_rows
    grad_attn = inv_rms * (
        grad_norm - normed * jnp.mean(grad_norm * normed, axis=-1, keepdims=True)
    )
    inner = jnp.sum(grad_attn * attn, axis=-1)
    base_low = (base_share[..., None] * grad_attn).astype(jnp.bfloat16)
    base_shift = -(base_share * inner)
    base_grad, base_soft = score_grads(q_own, k_own, v_own, base_total, base_low, base_shift)
    base_dq = query_part(base_grad, k_own)
    base_dk, base_dv = key_parts(base_grad, base_soft, q_own, base_low)
    mid_sel = pick_rows(mid_share[..., None], R1, mid_shift)[..., 0]
    mid_low = (mid_sel[..., None] * pick_rows(grad_attn, R1, mid_shift)).astype(jnp.bfloat16)
    mid_row_shift = -(mid_sel * pick_rows(inner[..., None], R1, mid_shift)[..., 0])
    mid_grad, mid_soft = score_grads(mid_q, mid_keys, mid_vals, mid_total, mid_low, mid_row_shift)
    mid_dq = query_part(mid_grad, mid_keys)
    mid_dk, mid_dv = key_parts(mid_grad, mid_soft, mid_q, mid_low)
    mid_dk = mid_dk.reshape(-1, flat_width)
    mid_dv = mid_dv.reshape(-1, flat_width)
    for level_bit in reversed(range(span_bits)):
        half_rows = mid_dk.shape[0] // 2
        upper_side = my_place >> level_bit & 1 == 1
        keep_k = jnp.where(upper_side, mid_dk[half_rows:], mid_dk[:half_rows])
        keep_v = jnp.where(upper_side, mid_dv[half_rows:], mid_dv[:half_rows])
        send_k = jnp.where(upper_side, mid_dk[:half_rows], mid_dk[half_rows:])
        send_v = jnp.where(upper_side, mid_dv[:half_rows], mid_dv[half_rows:])
        received = (
            swapped(send_k.astype(jnp.bfloat16), "ctx", level_bit).astype(send_k.dtype),
            swapped(send_v.astype(jnp.bfloat16), "ctx", level_bit).astype(send_v.dtype),
        )
        mid_dk = keep_k + received[0]
        mid_dv = keep_v + received[1]
    mid_dk = mid_dk.reshape(-1, head_count, HEAD_DIM)
    mid_dv = mid_dv.reshape(-1, head_count, HEAD_DIM)
    top_sel = pick_rows(top_share[..., None], ctx_size, top_shift)[..., 0]
    top_low = (top_sel[..., None] * pick_rows(grad_attn, ctx_size, top_shift)).astype(jnp.bfloat16)
    top_row_shift = -(top_sel * pick_rows(inner[..., None], ctx_size, top_shift)[..., 0])
    top_grad, top_soft = score_grads(top_q, top_keys, top_vals, top_total, top_low, top_row_shift)
    top_dq = query_part(top_grad, top_keys)
    gathered_dk, gathered_dv = key_parts(top_grad, top_soft, top_q, top_low)
    summed = (
        lax.psum_scatter(
            gathered_dk.reshape(-1, flat_width), "ctx", scatter_dimension=0, tiled=True
        ),
        lax.psum_scatter(
            gathered_dv.reshape(-1, flat_width), "ctx", scatter_dimension=0, tiled=True
        ),
    )
    top_dk = summed[0].reshape(-1, head_count, HEAD_DIM)
    top_dv = summed[1].reshape(-1, head_count, HEAD_DIM)
    query_grad = (
        base_dq + place_rows(mid_dq, R1, mid_shift) + place_rows(top_dq, ctx_size, top_shift)
    )
    key_grad = base_dk + place_rows(mid_dk, R1, mid_shift) + place_rows(top_dk, ctx_size, top_shift)
    value_grad = (
        base_dv + place_rows(mid_dv, R1, mid_shift) + place_rows(top_dv, ctx_size, top_shift)
    )
    out_shape = (1, tokens, flat_width)
    return (
        attended,
        query_grad.astype(jnp.bfloat16).reshape(out_shape),
        key_grad.astype(jnp.bfloat16).reshape(out_shape),
        value_grad.astype(jnp.bfloat16).reshape(out_shape),
        gain_grad,
    )


def solution(mesh):
    in_specs = (
        P("dp", "ctx", "head"),
        P("dp", "ctx", "head"),
        P("dp", "ctx", "head"),
        P("dp", "ctx", "head"),
        P("head"),
        P(None, "head"),
    )
    out_specs = (
        P("dp", "ctx", "head"),
        P("dp", "ctx", "head"),
        P("dp", "ctx", "head"),
        P("dp", "ctx", "head"),
        P("head"),
    )
    return jax.shard_map(shards, mesh=mesh, in_specs=in_specs, out_specs=out_specs, check_vma=False)
```

profile of v0, /device:TPU:266, one launch (start us, length us, event | category | flops | bytes accessed | tf_op | source)
XLA Modules:
  0.0 443.0 jit_solution(7934693849912801585)
XLA Ops:
  7.2 0.8 slice_bitcast_fusion.1
  8.0 1.5 fusion.26
  9.6 2.4 collective-permute-start
  12.0 3.6 collective-permute-start.2
  16.4 0.7 copy-done.2
  17.8 48.5 %all-gather = bf16[64,2,640]{2,1,0:T(2,128)(2,1)S(1)} all-gather(bf16[1,2,640]{2,1,0:T(2,128)(2,1)S(1)} %reshape.367), channel_id=1, replica_groups=mesh['dp'=2,'ctx'=64,'head'=4] {'ctx'}, dimensions={0}, use_global_device_ids=true | all-gather | bytes 166400 | tf_op jit(solution)/shard_map/all_gather | solution.py:117
  67.0 47.4 %all-gather.1 = bf16[64,2,640]{2,1,0:T(2,128)(2,1)S(1)} all-gather(bf16[1,2,640]{2,1,0:T(2,128)(2,1)S(1)} %reshape.369), channel_id=1, replica_groups=mesh['dp'=2,'ctx'=64,'head'=4] {'ctx'}, dimensions={0}, use_global_device_ids=true | all-gather | bytes 166400 | tf_op jit(solution)/shard_map/all_gather | solution.py:118
  114.6 0.3 fusion.60
  115.4 0.5 copy-done.4
  116.4 1.3 dynamic-slice
  118.4 4.6 %collective-permute-start.1 = (bf16[32,640]{1,0:T(8,128)(2,1)S(1)}, bf16[32,640]{1,0:T(8,128)(2,1)S(1)}, u32[]{:S(2)}, u32[]{:S(2)}) collective-permute-start(bf16[32,640]{1,0:T(8,128)(2,1)S(1)} %maximum_select_fusion.2), channel_id=1, source_target_pairs={{0,8},{8,0},{4,12},{12,4},{16,24},{24,16},{20,28},{28,20},{32,40},... | collective-permute-start | bytes 122888 | tf_op jit(solution)/shard_map/ppermute | solution.py:20
  123.0 2.2 collective-permute-start.3
  126.4 3.4 collective-permute-done.3
  130.0 0.5 multiply_reduce_fusion.3
  130.6 0.7 copy-done.5
  131.2 0.3 multiply_reduce_fusion
  133.0 1.0 fusion.50
  134.1 1.0 fusion.47
  135.1 0.4 fusion.14
  135.6 0.3 convolution_bitcast_fusion.4
  136.1 2.2 collective-permute-start.6
  138.7 4.6 %collective-permute-start.4 = (bf16[32,640]{1,0:T(8,128)(2,1)S(1)}, bf16[32,640]{1,0:T(8,128)(2,1)S(1)}, u32[]{:S(2)}, u32[]{:S(2)}) collective-permute-start(bf16[32,640]{1,0:T(8,128)(2,1)S(1)} %copy_bitcast_fusion.1), channel_id=1, source_target_pairs={{0,8},{8,0},{4,12},{12,4},{16,24},{24,16},{20,28},{28,20},{32,40},... | collective-permute-start | bytes 122888 | tf_op jit(solution)/shard_map/ppermute | solution.py:20
  143.4 0.8 copy.198
  144.3 275.7 %psum.7 = f32[640]{0:T(1024)} all-reduce(f32[640]{0:T(1024)S(1)} %bitcast.253), channel_id=1, replica_groups=mesh['dp'=2,'ctx'=64,'head'=4] {'dp','ctx'}, use_global_device_ids=true, to_apply=%region_24.25 | all-reduce | flops 640 | bytes 5120 | tf_op jit(solution)/shard_map/psum | solution.py:149
  420.0 4.7 %collective-permute-start.7 = (bf16[16,640]{1,0:T(8,128)(2,1)S(1)}, bf16[16,640]{1,0:T(8,128)(2,1)S(1)}, u32[]{:S(2)}, u32[]{:S(2)}) collective-permute-start(bf16[16,640]{1,0:T(8,128)(2,1)S(1)} %select_convert_fusion.2), channel_id=1, source_target_pairs={{0,4},{4,0},{8,12},{12,8},{16,20},{20,16},{24,28},{28,24},{32,36},... | collective-permute-start | bytes 61448 | tf_op jit(solution)/shard_map/ppermute | solution.py:20
  424.8 1.9 collective-permute-start.5
  426.8 3.7 collective-permute-done.5
  430.6 1.2 constant_dynamic-slice_fusion.1
  432.8 0.8 copy.200
  434.1 0.8 copy.199
  434.9 0.3 fusion.13
  435.4 0.8 copy.201
  (105 shorter events, 9.0 us)
Async XLA Ops:
  7.2 423.4 %all-reduce.5.cloned.1.call-start = ((), (), s32[]{:S(2)}) async-start(), calls=%async_computation | async-start | bytes 1310720
  8.0 7.6 %copy-start = (bf16[1,128,640]{2,1,0:T(8,128)(2,1)S(1)}, bf16[1,128,640]{2,1,0:T(8,128)(2,1)}, u32[]{:S(2)}) copy-start(bf16[1,128,640]{2,1,0:T(8,128)(2,1)} %param.6) | copy-start | bytes 491524
  9.6 108.7 %collective-permute-start = (bf16[16,640]{1,0:T(8,128)(2,1)S(1)}, bf16[16,640]{1,0:T(8,128)(2,1)S(1)}, u32[]{:S(2)}, u32[]{:S(2)}) collective-permute-start(bf16[16,640]{1,0:T(8,128)(2,1)S(1)} %copy_bitcast_fusion.7), channel_id=1, source_target_pairs={{0,4},{4,0},{8,12},{12,8},{16,20},{20,16},{24,28},{28,24},{32,36},... | collective-permute-start | bytes 61448 | tf_op jit(solution)/shard_map/ppermute | solution.py:20
  12.0 3.8 copy-start.1
  12.0 106.4 %collective-permute-start.2 = (bf16[16,640]{1,0:T(8,128)(2,1)S(1)}, bf16[16,640]{1,0:T(8,128)(2,1)S(1)}, u32[]{:S(2)}, u32[]{:S(2)}) collective-permute-start(bf16[16,640]{1,0:T(8,128)(2,1)S(1)} %copy_bitcast_fusion.6), channel_id=1, source_target_pairs={{0,4},{4,0},{8,12},{12,8},{16,20},{20,16},{24,28},{28,24},{32,36},... | collective-permute-start | bytes 61448 | tf_op jit(solution)/shard_map/ppermute | solution.py:20
  16.2 0.9 copy-start.2
  115.0 0.9 copy-start.4
  118.4 6.9 %collective-permute-start.1 = (bf16[32,640]{1,0:T(8,128)(2,1)S(1)}, bf16[32,640]{1,0:T(8,128)(2,1)S(1)}, u32[]{:S(2)}, u32[]{:S(2)}) collective-permute-start(bf16[32,640]{1,0:T(8,128)(2,1)S(1)} %maximum_select_fusion.2), channel_id=1, source_target_pairs={{0,8},{8,0},{4,12},{12,4},{16,24},{24,16},{20,28},{28,20},{32,40},... | collective-permute-start | bytes 122888 | tf_op jit(solution)/shard_map/ppermute | solution.py:20
  123.0 6.8 %collective-permute-start.3 = (bf16[32,640]{1,0:T(8,128)(2,1)S(1)}, bf16[32,640]{1,0:T(8,128)(2,1)S(1)}, u32[]{:S(2)}, u32[]{:S(2)}) collective-permute-start(bf16[32,640]{1,0:T(8,128)(2,1)S(1)} %maximum_select_fusion.4), channel_id=1, source_target_pairs={{0,8},{8,0},{4,12},{12,4},{16,24},{24,16},{20,28},{28,20},{32,40},... | collective-permute-start | bytes 122888 | tf_op jit(solution)/shard_map/ppermute | solution.py:20
  130.5 0.7 copy-start.5
  136.1 283.9 %collective-permute-start.6 = (bf16[32,640]{1,0:T(8,128)(2,1)S(1)}, bf16[32,640]{1,0:T(8,128)(2,1)S(1)}, u32[]{:S(2)}, u32[]{:S(2)}) collective-permute-start(bf16[32,640]{1,0:T(8,128)(2,1)S(1)} %copy_bitcast_fusion), channel_id=1, source_target_pairs={{0,8},{8,0},{4,12},{12,4},{16,24},{24,16},{20,28},{28,20},{32,40},... | collective-permute-start | bytes 122888 | tf_op jit(solution)/shard_map/ppermute | solution.py:20
  138.7 286.1 %collective-permute-start.4 = (bf16[32,640]{1,0:T(8,128)(2,1)S(1)}, bf16[32,640]{1,0:T(8,128)(2,1)S(1)}, u32[]{:S(2)}, u32[]{:S(2)}) collective-permute-start(bf16[32,640]{1,0:T(8,128)(2,1)S(1)} %copy_bitcast_fusion.1), channel_id=1, source_target_pairs={{0,8},{8,0},{4,12},{12,4},{16,24},{24,16},{20,28},{28,20},{32,40},... | collective-permute-start | bytes 122888 | tf_op jit(solution)/shard_map/ppermute | solution.py:20
  420.0 6.7 %collective-permute-start.7 = (bf16[16,640]{1,0:T(8,128)(2,1)S(1)}, bf16[16,640]{1,0:T(8,128)(2,1)S(1)}, u32[]{:S(2)}, u32[]{:S(2)}) collective-permute-start(bf16[16,640]{1,0:T(8,128)(2,1)S(1)} %select_convert_fusion.2), channel_id=1, source_target_pairs={{0,4},{4,0},{8,12},{12,8},{16,20},{20,16},{24,28},{28,24},{32,36},... | collective-permute-start | bytes 61448 | tf_op jit(solution)/shard_map/ppermute | solution.py:20
  424.8 5.7 %collective-permute-start.5 = (bf16[16,640]{1,0:T(8,128)(2,1)S(1)}, bf16[16,640]{1,0:T(8,128)(2,1)S(1)}, u32[]{:S(2)}, u32[]{:S(2)}) collective-permute-start(bf16[16,640]{1,0:T(8,128)(2,1)S(1)} %select_convert_fusion.3), channel_id=1, source_target_pairs={{0,4},{4,0},{8,12},{12,8},{16,20},{20,16},{24,28},{28,24},{32,36},... | collective-permute-start | bytes 61448 | tf_op jit(solution)/shard_map/ppermute | solution.py:20
  430.6 1.2 copy-start.3
Sparse Core Ops, SparseCore 0:
  144.4 154.0 all-reduce.4
where the time goes:
time: 444 us; the launch traced here: 443 us
  blocking collectives  372 us (84%)
  starting transfers between devices  26.2 us (6%)
  between operations  15.2 us (3%)
  local copies, waits for them, and re-layouts  12.3 us (3%)
  waiting for transfers between devices  7.26 us (2%)
  matrix products  6.13 us (1%)
    psum x1, blocking collectives, shards(): gain_grad = lax.psum(gain_part, ('dp', 'ctx'))  276 us
    all_gather x1, blocking collectives, shards(): lax.all_gather(top_keys, 'ctx', axis=0, tiled=True)  48.5 us
    all_gather x1, blocking collectives, shards(): lax.all_gather(top_vals, 'ctx', axis=0, tiled=True)  47.4 us
    ppermute x8, starting transfers between devices, swapped(): return lax.ppermute(block, axis, route)  26.1 us
  transfers between devices with their start and end apart: 9, of which 3 were waited for; matrix products, arithmetic and copies ran while one was open for 2% of the time, Pallas kernels for 0%

commit v1 on v0

--- a/solution.py
+++ b/solution.py
@@ -146,7 +146,7 @@
     attended = (normed * gain_rows).astype(jnp.bfloat16).reshape(1, tokens, flat_width)
     grad_full = grad_y[0].reshape(row_shape).astype(jnp.float32)
     gain_part = jnp.sum(grad_full * normed, axis=0).reshape(flat_width)
-    gain_grad = lax.psum(gain_part, ("dp", "ctx"))
+    gain_grad = jnp.sum(lax.all_gather(gain_part, ("dp", "ctx")), axis=0)
     grad_norm = grad_full * gain_rows
     grad_attn = inv_rms * (
         grad_norm - normed * jnp.mean(grad_norm * normed, axis=-1, keepdims=True)

time: 444 us -> 589 us (1.33)
  the two profiles are of different devices: /device:TPU:266 before, /device:TPU:2 now
where the time goes in v1:
time: 589 us
  blocking collectives  351 us (60%)
  waiting for transfers between devices  174 us (30%)
  starting transfers between devices  25.3 us (4%)
  between operations  15.2 us (3%)
  local copies, waits for them, and re-layouts  12.3 us (2%)
  matrix products  6.16 us (1%)
    all_gather x1, blocking collectives, shards(): gain_grad = jnp.sum(lax.all_gather(gain_part, ('dp', 'ctx')), axis=0)  247 us
    unnamed x2, waiting for transfers between devices  170 us
    all_gather x1, blocking collectives, shards(): lax.all_gather(top_keys, 'ctx', axis=0, tiled=True)  56.5 us
    all_gather x1, blocking collectives, shards(): lax.all_gather(top_vals, 'ctx', axis=0, tiled=True)  47.7 us
    ppermute x8, starting transfers between devices, swapped(): return lax.ppermute(block, axis, route)  25.3 us
  transfers between devices with their start and end apart: 9, of which 4 were waited for; matrix products, arithmetic and copies ran while one was open for 1% of the time, Pallas kernels for 0%

profile of v1, /device:TPU:2, one launch (start us, length us, event | category | flops | bytes accessed | tf_op | source)
XLA Modules:
  0.0 588.7 jit_solution(11819830100013709013)
XLA Ops:
  7.2 0.8 slice_bitcast_fusion.1
  8.0 1.5 fusion.26
  9.6 3.5 collective-permute-start
  13.1 2.5 collective-permute-start.2
  16.4 0.7 copy-done.2
  17.8 56.5 %all-gather = bf16[64,2,640]{2,1,0:T(2,128)(2,1)S(1)} all-gather(bf16[1,2,640]{2,1,0:T(2,128)(2,1)S(1)} %reshape.363), channel_id=1, replica_groups=mesh['dp'=2,'ctx'=64,'head'=4] {'ctx'}, dimensions={0}, use_global_device_ids=true | all-gather | bytes 166400 | tf_op jit(solution)/shard_map/all_gather | solution.py:117
  75.0 47.7 %all-gather.1 = bf16[64,2,640]{2,1,0:T(2,128)(2,1)S(1)} all-gather(bf16[1,2,640]{2,1,0:T(2,128)(2,1)S(1)} %reshape.365), channel_id=1, replica_groups=mesh['dp'=2,'ctx'=64,'head'=4] {'ctx'}, dimensions={0}, use_global_device_ids=true | all-gather | bytes 166400 | tf_op jit(solution)/shard_map/all_gather | solution.py:118
  123.7 0.5 copy-done.4
  124.7 1.3 dynamic-slice
  126.7 2.7 collective-permute-start.1
  129.5 4.0 collective-permute-start.3
  133.5 0.5 collective-permute-done.1
  135.1 1.2 collective-permute-done.3
  136.5 0.5 multiply_reduce_fusion.3
  137.1 0.7 copy-done.5
  138.8 0.3 convolution_bitcast_fusion.4
  140.6 1.0 fusion.50
  141.6 1.0 fusion.47
  142.6 0.4 fusion.14
  143.0 4.0 collective-permute-start.6
  147.0 2.7 collective-permute-start.4
  149.8 246.8 %all-gather.2 = f32[128,1,640]{2,1,0:T(1,128)S(1)} all-gather(f32[1,1,640]{2,1,0:T(1,128)S(1)} %reshape.367), channel_id=1, replica_groups=mesh['dp'=2,'ctx'=64,'head'=4] {'dp','ctx'}, dimensions={0}, use_global_device_ids=true | all-gather | bytes 330240 | tf_op jit(solution)/shard_map/all_gather | solution.py:149
  396.7 0.8 copy.198
  397.6 0.8 reduce_sum.199
  398.5 1.9 collective-permute-start.7
  400.4 3.9 collective-permute-start.5
  404.4 1.7 collective-permute-done.5
  406.1 170.2 %all-reduce.5.cloned.1.call-done = (f32[128,640]{0,1:T(8,128)}, f32[128,640]{0,1:T(8,128)}) async-done(((f32[128,640]{0,1:T(8,128)}, f32[128,640]{0,1:T(8,128)}), (f32[128,640]{0,1:T(8,128)}, f32[128,640]{0,1:T(8,128)})) %all-reduce.5.cloned.1.call-update) | async-done | bytes 655376
  576.3 1.2 constant_dynamic-slice_fusion.1
  578.5 0.8 copy.200
  579.8 0.8 copy.199
  581.1 0.8 copy.201
  (107 shorter events, 9.8 us)
Async XLA Ops:
  7.2 569.1 %all-reduce.5.cloned.1.call-start = ((), (), s32[]{:S(2)}) async-start(), calls=%async_computation | async-start | bytes 1310720
  8.0 7.6 %copy-start = (bf16[1,128,640]{2,1,0:T(8,128)(2,1)S(1)}, bf16[1,128,640]{2,1,0:T(8,128)(2,1)}, u32[]{:S(2)}) copy-start(bf16[1,128,640]{2,1,0:T(8,128)(2,1)} %param.6) | copy-start | bytes 491524
  9.6 117.0 %collective-permute-start = (bf16[16,640]{1,0:T(8,128)(2,1)S(1)}, bf16[16,640]{1,0:T(8,128)(2,1)S(1)}, u32[]{:S(2)}, u32[]{:S(2)}) collective-permute-start(bf16[16,640]{1,0:T(8,128)(2,1)S(1)} %copy_bitcast_fusion.7), channel_id=1, source_target_pairs={{0,4},{4,0},{8,12},{12,8},{16,20},{20,16},{24,28},{28,24},{32,36},... | collective-permute-start | bytes 61448 | tf_op jit(solution)/shard_map/ppermute | solution.py:20
  13.1 2.7 copy-start.1
  13.1 113.6 %collective-permute-start.2 = (bf16[16,640]{1,0:T(8,128)(2,1)S(1)}, bf16[16,640]{1,0:T(8,128)(2,1)S(1)}, u32[]{:S(2)}, u32[]{:S(2)}) collective-permute-start(bf16[16,640]{1,0:T(8,128)(2,1)S(1)} %copy_bitcast_fusion.6), channel_id=1, source_target_pairs={{0,4},{4,0},{8,12},{12,8},{16,20},{20,16},{24,28},{28,24},{32,36},... | collective-permute-start | bytes 61448 | tf_op jit(solution)/shard_map/ppermute | solution.py:20
  16.2 0.9 copy-start.2
  123.3 0.9 copy-start.4
  126.7 7.2 %collective-permute-start.1 = (bf16[32,640]{1,0:T(8,128)(2,1)S(1)}, bf16[32,640]{1,0:T(8,128)(2,1)S(1)}, u32[]{:S(2)}, u32[]{:S(2)}) collective-permute-start(bf16[32,640]{1,0:T(8,128)(2,1)S(1)} %maximum_select_fusion.2), channel_id=1, source_target_pairs={{0,8},{8,0},{4,12},{12,4},{16,24},{24,16},{20,28},{28,20},{32,40},... | collective-permute-start | bytes 122888 | tf_op jit(solution)/shard_map/ppermute | solution.py:20
  129.5 6.8 %collective-permute-start.3 = (bf16[32,640]{1,0:T(8,128)(2,1)S(1)}, bf16[32,640]{1,0:T(8,128)(2,1)S(1)}, u32[]{:S(2)}, u32[]{:S(2)}) collective-permute-start(bf16[32,640]{1,0:T(8,128)(2,1)S(1)} %maximum_select_fusion.4), channel_id=1, source_target_pairs={{0,8},{8,0},{4,12},{12,4},{16,24},{24,16},{20,28},{28,20},{32,40},... | collective-permute-start | bytes 122888 | tf_op jit(solution)/shard_map/ppermute | solution.py:20
  137.0 0.7 copy-start.5
  143.0 255.4 %collective-permute-start.6 = (bf16[32,640]{1,0:T(8,128)(2,1)S(1)}, bf16[32,640]{1,0:T(8,128)(2,1)S(1)}, u32[]{:S(2)}, u32[]{:S(2)}) collective-permute-start(bf16[32,640]{1,0:T(8,128)(2,1)S(1)} %copy_bitcast_fusion), channel_id=1, source_target_pairs={{0,8},{8,0},{4,12},{12,4},{16,24},{24,16},{20,28},{28,20},{32,40},... | collective-permute-start | bytes 122888 | tf_op jit(solution)/shard_map/ppermute | solution.py:20
  147.0 253.3 %collective-permute-start.4 = (bf16[32,640]{1,0:T(8,128)(2,1)S(1)}, bf16[32,640]{1,0:T(8,128)(2,1)S(1)}, u32[]{:S(2)}, u32[]{:S(2)}) collective-permute-start(bf16[32,640]{1,0:T(8,128)(2,1)S(1)} %copy_bitcast_fusion.1), channel_id=1, source_target_pairs={{0,8},{8,0},{4,12},{12,4},{16,24},{24,16},{20,28},{28,20},{32,40},... | collective-permute-start | bytes 122888 | tf_op jit(solution)/shard_map/ppermute | solution.py:20
  398.5 5.9 %collective-permute-start.7 = (bf16[16,640]{1,0:T(8,128)(2,1)S(1)}, bf16[16,640]{1,0:T(8,128)(2,1)S(1)}, u32[]{:S(2)}, u32[]{:S(2)}) collective-permute-start(bf16[16,640]{1,0:T(8,128)(2,1)S(1)} %select_convert_fusion.2), channel_id=1, source_target_pairs={{0,4},{4,0},{8,12},{12,8},{16,20},{20,16},{24,28},{28,24},{32,36},... | collective-permute-start | bytes 61448 | tf_op jit(solution)/shard_map/ppermute | solution.py:20
  400.4 5.7 collective-permute-start.5
  576.3 1.2 copy-start.3
Sparse Core Ops, SparseCore 0:
  397.7 178.5 all-reduce.4
